TPU v7x, 256 devices: a whole 4x4x8 slice. The times are simulated.
256 devices in a mesh: ent: 64 (over z, y, core), rel: 4 (over x).
Axes of the slice: x: 4, y: 4, z: 8, core: 2. Of those that a mesh axis runs over, the one named last changes fastest.
Arguments:
- entity_rows: bfloat16 [65536, 256], P('ent'), may hold values from -2.5 to 2.5
- request_rows: int32 [64, 64, 32], P('ent'), may hold values from 0 to 1023
- edge_heads: int32 [262144], P(('ent', 'rel')), may hold values from 0 to 1023
- edge_rels: int32 [262144], P(('ent', 'rel')), may hold values from 0 to 7
- edge_tails: int32 [262144], P(('ent', 'rel')), may hold values from 0 to 2047
- edge_counts: int32 [256], P(('ent', 'rel')), may hold values from 1 to 1024, 163840 in all
- negative_rows: int32 [65536], P(('ent', 'rel')), may hold values from 0 to 1023
- relation_blocks: bfloat16 [32, 8, 32, 32], P('rel'), may hold values from -1 to 1
Outputs:
- entity_grad: float32 [65536, 256], P('ent')
- relation_grad: float32 [32, 8, 32, 32], P('rel')
Inputs may be any that keep to these rules, and one draw needn't show every extreme that they name: Edge slots of bucket b at or past edge_counts[b] are ignored; some bucket is full in every draw.
All inputs are finite; a program needn't handle non-finite values. No bound on the sum of `edge_counts` on one device may be relied on, other than what follows from the above.
Results may differ from a plain program's by a relative error of at most 0.009.
Values may be sent and summed in bfloat16 or wider, within the bound.
No kernel may reach another device: no remote copies, remote signals or barrier semaphores. Data moves between devices by JAX's collectives and lax.ppermute only.
A program may use at most 64 MiB of HBM per device.

v0:
```python
import math
import jax
import jax.numpy as jnp
from jax import lax
from jax.sharding import PartitionSpec as P


def pick_rows(indices, source_table):
    row_total = indices.shape[0]
    block_size = math.gcd(row_total, 256)
    grouped = indices.reshape(row_total // block_size, block_size)
    columns = jnp.arange(source_table.shape[0], dtype=jnp.int32)

    def pick_block(index_block):
        one_hot = (index_block[:, None] == columns[None, :]).astype(jnp.bfloat16)
        return jnp.dot(one_hot, source_table, preferred_element_type=jnp.float32).astype(
            jnp.bfloat16
        )

    picked = lax.map(pick_block, grouped)
    return picked.reshape(row_total, source_table.shape[1])


def owner_add(indices, gradients, entity_count):
    start_value = jnp.zeros((entity_count, gradients.shape[1]), jnp.float32)
    return start_value.at[indices].add(gradients)


def local(
    entity_rows,
    request_rows,
    edge_heads,
    edge_rels,
    edge_tails,
    edge_counts,
    negative_rows,
    relation_blocks,
):
    entity_count, feature_width = entity_rows.shape
    part_count = request_rows.shape[1]
    slot_count = request_rows.shape[2]
    r_count, block_count, block_width = (
        relation_blocks.shape[0],
        relation_blocks.shape[1],
        relation_blocks.shape[2],
    )
    neg_count = negative_rows.shape[0]
    owner_lists = lax.all_to_all(request_rows, "ent", split_axis=1, concat_axis=0, tiled=True)
    wanted = pick_rows(owner_lists.reshape(-1), entity_rows).reshape(
        part_count, 1, slot_count, feature_width
    )
    fetched = lax.all_to_all(wanted, "ent", split_axis=0, concat_axis=1, tiled=True)
    fetched = fetched.reshape(part_count * slot_count, feature_width)
    neg_rows = pick_rows(negative_rows, entity_rows)
    edge_dev = edge_heads.shape[0]
    block_size = math.gcd(edge_dev, 256)
    block_total = edge_dev // block_size
    live_count = edge_counts[0]
    positions = jnp.arange(edge_dev, dtype=jnp.int32).reshape(block_total, block_size)
    entity_columns = jnp.arange(entity_count, dtype=jnp.int32)
    slot_columns = jnp.arange(part_count * slot_count, dtype=jnp.int32)
    rel_columns = jnp.arange(r_count, dtype=jnp.int32)
    contract_rows = (((0,), (0,)), ((), ()))

    def edge_block(running, block_inputs):
        slot_acc, entity_acc, neg_acc, relation_acc = running
        head_ids, rel_ids, tail_ids, places = block_inputs
        live_mask = (places < live_count).astype(jnp.float32)
        head_hot = (head_ids[:, None] == entity_columns[None, :]).astype(jnp.bfloat16)
        tail_hot = (tail_ids[:, None] == slot_columns[None, :]).astype(jnp.bfloat16)
        head_rows = jnp.dot(head_hot, entity_rows, preferred_element_type=jnp.float32).astype(
            jnp.bfloat16
        )
        tail_rows = jnp.dot(tail_hot, fetched, preferred_element_type=jnp.float32).astype(
            jnp.bfloat16
        )
        rel_hot = (rel_ids[:, None] == rel_columns[None, :]).astype(jnp.float32)
        head_split = head_rows.reshape(block_size, block_count, block_width)
        proj_all = jnp.einsum(
            "enb,rnbc->renc", head_split, relation_blocks, preferred_element_type=jnp.float32
        )
        projected = (
            jnp.sum(rel_hot.T[:, :, None, None] * proj_all, 0)
            .reshape(block_size, feature_width)
            .astype(jnp.bfloat16)
        )
        projected_wide = projected.astype(jnp.float32)
        positive = jnp.sum(projected_wide * tail_rows.astype(jnp.float32), -1)
        negative = lax.dot_general(
            projected, neg_rows, (((1,), (1,)), ((), ())), preferred_element_type=jnp.float32
        )
        pos_weight = -live_mask * jax.nn.sigmoid(-positive)
        neg_weight = (live_mask[:, None] * jax.nn.sigmoid(negative) / neg_count).astype(
            jnp.bfloat16
        )
        grad_proj = (
            pos_weight[:, None] * tail_rows.astype(jnp.float32)
            + jnp.dot(neg_weight, neg_rows, preferred_element_type=jnp.float32)
        ).astype(jnp.bfloat16)
        weighted = (pos_weight[:, None] * projected_wide).astype(jnp.bfloat16)
        grad_split = grad_proj.reshape(block_size, block_count, block_width)
        back_all = jnp.einsum(
            "enc,rnbc->renb", grad_split, relation_blocks, preferred_element_type=jnp.float32
        )
        head_grad = (
            jnp.sum(rel_hot.T[:, :, None, None] * back_all, 0)
            .reshape(block_size, feature_width)
            .astype(jnp.bfloat16)
        )
        slot_acc = slot_acc + lax.dot_general(
            tail_hot, weighted, contract_rows, preferred_element_type=jnp.float32
        )
        entity_acc = entity_acc + lax.dot_general(
            head_hot, head_grad, contract_rows, preferred_element_type=jnp.float32
        )
        neg_acc = neg_acc + lax.dot_general(
            neg_weight, projected, contract_rows, preferred_element_type=jnp.float32
        )
        masked_heads = rel_hot.T.astype(jnp.bfloat16)[:, :, None, None] * head_split[None]
        relation_acc = relation_acc + jnp.einsum(
            "renb,enc->rnbc", masked_heads, grad_split, preferred_element_type=jnp.float32
        )
        return ((slot_acc, entity_acc, neg_acc, relation_acc), None)

    start_values = (
        jnp.zeros((part_count * slot_count, feature_width), jnp.float32),
        jnp.zeros((entity_count, feature_width), jnp.float32),
        jnp.zeros((neg_count, feature_width), jnp.float32),
        jnp.zeros(relation_blocks.shape, jnp.float32),
    )
    block_inputs = (
        edge_heads.reshape(block_total, block_size),
        edge_rels.reshape(block_total, block_size),
        edge_tails.reshape(block_total, block_size),
        positions,
    )
    (slot_acc, entity_acc, neg_acc, relation_acc), _ = lax.scan(
        edge_block, start_values, block_inputs
    )
    neg_hot = (negative_rows[:, None] == entity_columns[None, :]).astype(jnp.bfloat16)
    entity_acc = entity_acc + lax.dot_general(
        neg_hot, neg_acc.astype(jnp.bfloat16), contract_rows, preferred_element_type=jnp.float32
    )
    slot_grads = slot_acc.reshape(1, part_count, slot_count, feature_width)
    returned = lax.all_to_all(
        slot_grads.astype(jnp.bfloat16), "ent", split_axis=1, concat_axis=0, tiled=True
    ).astype(slot_grads.dtype)
    entity_acc = entity_acc + owner_add(
        owner_lists.reshape(-1), returned.reshape(-1, feature_width), entity_count
    )
    entity_grad = lax.psum(entity_acc, "rel")
    relation_grad = lax.psum(relation_acc, "ent")
    return (entity_grad, relation_grad)


def solution(mesh):
    in_specs = (
        P("ent", None),
        P("ent", None, None),
        P(("ent", "rel")),
        P(("ent", "rel")),
        P(("ent", "rel")),
        P(("ent", "rel")),
        P(("ent", "rel")),
        P("rel", None, None, None),
    )
    out_specs = (P("ent", None), P("rel", None, None, None))
    return jax.shard_map(local, mesh=mesh, in_specs=in_specs, out_specs=out_specs, check_vma=False)
```

profile of v0, /device:TPU:8, one launch (start us, length us, event | category | flops | bytes accessed | tf_op | source)
XLA Modules:
  0.0 383.0 jit_solution(16212449031649504692)
XLA Ops:
  8.6 12.1 %all-to-all-start = ((s32[1,64,32]{2,0,1:T(1,128)}), s32[1,64,32]{2,0,1:T(1,128)S(1)}, u32[]{:S(2)}, u32[]{:S(2)}) async-start(s32[1,64,32]{2,0,1:T(1,128)} %copy.20), calls=%async_computation | async-start | bytes 65536 | tf_op jit(solution)/shard_map/all_to_all | solution.py:48
  20.7 8.5 %all-to-all-done = s32[1,64,32]{2,0,1:T(1,128)S(1)} async-done(((s32[1,64,32]{2,0,1:T(1,128)}), s32[1,64,32]{2,0,1:T(1,128)S(1)}, u32[]{:S(2)}, u32[]{:S(2)}) %all-to-all-start) | async-done | bytes 8224 | tf_op jit(solution)/shard_map/all_to_all | solution.py:48
  30.6 16.5 %while.32 = (s32[]{:T(128)}, bf16[8,256,256]{2,1,0:T(8,128)(2,1)}, s32[8,256]{1,0:T(8,128)S(1)}, bf16[1024,256]{1,0:T(8,128)(2,1)}, s32[]{:T(128)}) while((s32[]{:T(128)}, bf16[8,256,256]{2,1,0:T(8,128)(2,1)}, s32[8,256]{1,0:T(8,128)S(1)}, bf16[1024,256]{1,0:T(8,128)(2,1)}, s32[]{:T(128)}) %tuple.56), condition=%wide.region_1.2_spmd.clone, body=%wide.region_0.1_spmd.clone.sunk | while | flops 134545408 | bytes 658509 | solution.py:20
  30.6 2.1 fusion.90
  32.6 2.0 fusion.90
  34.7 2.0 fusion.90
  36.8 2.1 fusion.90
  38.8 2.1 fusion.90
  40.9 2.0 fusion.90
  42.9 2.0 fusion.90
  45.0 2.1 fusion.90
  47.0 6.5 %all-to-all-start.1 = ((bf16[64,1,32,256]{3,2,1,0:T(8,128)(2,1)}), bf16[64,1,32,256]{3,2,1,0:T(8,128)(2,1)}, u32[]{:S(2)}, u32[]{:S(2)}) async-start(bf16[64,1,32,256]{3,2,1,0:T(8,128)(2,1)} %bitcast.1), calls=%async_computation.1 | async-start | bytes 2097152 | tf_op jit(solution)/shard_map/all_to_all | solution.py:52
  56.9 25.4 %all-to-all-done.1 = bf16[64,1,32,256]{3,2,1,0:T(8,128)(2,1)} async-done(((bf16[64,1,32,256]{3,2,1,0:T(8,128)(2,1)}), bf16[64,1,32,256]{3,2,1,0:T(8,128)(2,1)}, u32[]{:S(2)}, u32[]{:S(2)}) %all-to-all-start.1) | async-done | bytes 1048608 | tf_op jit(solution)/shard_map/all_to_all | solution.py:52
  82.3 38.9 %while.33 = (s32[]{:T(128)}, f32[2048,256]{1,0:T(8,128)S(1)}, f32[1024,256]{1,0:T(8,128)S(1)}, f32[256,256]{1,0:T(8,128)S(1)}, f32[8,8,32,32]{2,3,0,1:T(8,128)},...) while((s32[]{:T(128)}, f32[2048,256]{1,0:T(8,128)S(1)}, ...), condition=%wide.region_6.7_spmd.clone, body=%wide.region_2.6_spmd.clone.sunk | while | flops 1016077568 | bytes 14733582 | solution.py:137
  86.6 2.1 fusion.111
  96.4 2.1 fusion.111
  106.1 2.1 fusion.111
  115.8 2.1 fusion.111
  122.3 5.9 %all-to-all-start.2 = ((bf16[1,64,32,256]{3,2,0,1:T(8,128)(2,1)}), bf16[1,64,32,256]{3,2,0,1:T(8,128)(2,1)S(1)}, u32[]{:S(2)}, u32[]{:S(2)}) async-start(bf16[1,64,32,256]{3,2,0,1:T(8,128)(2,1)} %bitcast.124), calls=%async_computation.2 | async-start | bytes 2097152 | tf_op jit(solution)/shard_map/all_to_all | solution.py:145
  130.4 27.4 %all-to-all-done.2 = bf16[1,64,32,256]{3,2,0,1:T(8,128)(2,1)S(1)} async-done(((bf16[1,64,32,256]{3,2,0,1:T(8,128)(2,1)}), bf16[1,64,32,256]{3,2,0,1:T(8,128)(2,1)S(1)}, u32[]{:S(2)}, u32[]{:S(2)}) %all-to-all-start.2) | async-done | bytes 1048608 | tf_op jit(solution)/shard_map/all_to_all | solution.py:145
  157.7 12.0 %scatter_custom_fusion = f32[1024,256]{1,0:T(8,128)S(1)} fusion(f32[1024,256]{1,0:T(8,128)S(1)} %convolution_add_fusion.4, s32[2048]{0:T(1024)S(1)} %bitcast.138, bf16[2048,256]{1,0:T(8,128)(2,1)S(1)} %bitcast.125), kind=kCustom, calls=%fused_computation.57 | custom fusion | flops 1048576 | bytes 2097152 | tf_op jit(solution)/shard_map/scatter-add | solution.py:26
  170.8 150.9 %all-reduce.5.cloned.1.call-done = f32[8,8,32,32]{3,2,1,0:T(8,128)} async-done(((f32[8,8,32,32]{3,2,1,0:T(8,128)}), f32[8,8,32,32]{3,2,1,0:T(8,128)}) %all-reduce.5.cloned.1.call-update) | async-done | bytes 262160 | tf_op jit(solution)/shard_map/psum | solution.py:152
  321.6 51.3 %all-reduce.3.cloned.1.call-done = f32[1024,256]{1,0:T(8,128)} async-done(((f32[1024,256]{1,0:T(8,128)}), f32[1024,256]{1,0:T(8,128)}) %all-reduce.3.cloned.1.call-update) | async-done | bytes 1048592 | tf_op jit(solution)/shard_map/psum | solution.py:151
  372.9 2.3 copy.51
  (131 shorter events, 41.3 us)
Async XLA Ops:
  8.6 20.7 %all-to-all-start = ((s32[1,64,32]{2,0,1:T(1,128)}), s32[1,64,32]{2,0,1:T(1,128)S(1)}, u32[]{:S(2)}, u32[]{:S(2)}) async-start(s32[1,64,32]{2,0,1:T(1,128)} %copy.20), calls=%async_computation | async-start | bytes 65536 | tf_op jit(solution)/shard_map/all_to_all | solution.py:48
  47.0 6.5 %copy-start.8 = (s32[1024]{0:T(1024)S(1)}, s32[1024]{0:T(1024)}, u32[]{:S(2)}) copy-start(s32[1024]{0:T(1024)} %param.14) | copy-start | bytes 12292
  47.0 6.5 %copy-start.9 = (s32[1024]{0:T(1024)S(1)}, s32[1024]{0:T(1024)}, u32[]{:S(2)}) copy-start(s32[1024]{0:T(1024)} %param.15) | copy-start | bytes 12292
  47.0 6.6 %copy-start.10 = (s32[1024]{0:T(1024)S(1)}, s32[1024]{0:T(1024)}, u32[]{:S(2)}) copy-start(s32[1024]{0:T(1024)} %param.16) | copy-start | bytes 12292
  47.0 35.3 %all-to-all-start.1 = ((bf16[64,1,32,256]{3,2,1,0:T(8,128)(2,1)}), bf16[64,1,32,256]{3,2,1,0:T(8,128)(2,1)}, u32[]{:S(2)}, u32[]{:S(2)}) async-start(bf16[64,1,32,256]{3,2,1,0:T(8,128)(2,1)} %bitcast.1), calls=%async_computation.1 | async-start | bytes 2097152 | tf_op jit(solution)/shard_map/all_to_all | solution.py:52
  86.4 2.6 copy-start.5
  86.6 2.8 copy-start
  90.4 1.7 copy-start.1
  96.1 2.6 copy-start.5
  96.4 2.8 copy-start
  100.1 1.7 copy-start.1
  105.8 2.6 copy-start.5
  106.1 2.8 copy-start
  109.8 1.7 copy-start.1
  115.6 2.6 copy-start.5
  115.8 2.8 copy-start
  119.6 1.7 copy-start.1
  121.2 7.0 %copy-start.7 = (s32[1,64,32]{2,0,1:T(1,128)S(1)}, s32[1,64,32]{2,0,1:T(1,128)}, u32[]{:S(2)}) copy-start(s32[1,64,32]{2,0,1:T(1,128)} %copy-done.6) | copy-start | bytes 24580
  122.3 6.0 %copy-start.2 = (f32[8,8,32,32]{2,3,0,1:T(8,128)S(1)}, f32[8,8,32,32]{2,3,0,1:T(8,128)}, u32[]{:S(2)}) copy-start(f32[8,8,32,32]{2,3,0,1:T(8,128)} %get-tuple-element.138) | copy-start | bytes 786436
  122.3 35.4 %all-to-all-start.2 = ((bf16[1,64,32,256]{3,2,0,1:T(8,128)(2,1)}), bf16[1,64,32,256]{3,2,0,1:T(8,128)(2,1)S(1)}, u32[]{:S(2)}, u32[]{:S(2)}) async-start(bf16[1,64,32,256]{3,2,0,1:T(8,128)(2,1)} %bitcast.124), calls=%async_computation.2 | async-start | bytes 2097152 | tf_op jit(solution)/shard_map/all_to_all | solution.py:145
  128.2 1.6 copy-start.11
  128.2 193.4 %all-reduce.5.cloned.1.call-start = ((), (), s32[]{:S(2)}) async-start(), calls=%async_computation.4 | async-start | bytes 2097152 | tf_op jit(solution)/shard_map/psum | solution.py:152
  129.8 243.2 %all-reduce.3.cloned.1.call-start = ((), (), s32[]{:S(2)}) async-start(), calls=%async_computation.3 | async-start | bytes 2097152 | tf_op jit(solution)/shard_map/psum | solution.py:151
  321.6 53.6 %copy-start.4 = (f32[8,8,32,32]{3,2,1,0:T(8,128)S(1)}, f32[8,8,32,32]{3,2,1,0:T(8,128)}, u32[]{:S(2)}) copy-start(f32[8,8,32,32]{3,2,1,0:T(8,128)} %all-reduce.5.cloned.1.call-done) | copy-start | bytes 786436
  (2 other events, 2.3 us)
Sparse Core Ops, SparseCore 0:
  132.4 189.1 all-reduce.4
  324.6 48.3 all-reduce.2
where the time goes:
time: 384 us; the launch traced here: 383 us
  waiting for transfers between devices  263 us (68%)
  matrix products  53.8 us (14%)
  starting transfers between devices  24.5 us (6%)
  other arithmetic  16.5 us (4%)
  between operations  14.2 us (4%)
  local copies, waits for them, and re-layouts  9.81 us (3%)
    psum x1, waiting for transfers between devices, local(): relation_grad = lax.psum(relation_acc, 'ent')  151 us
    psum x1, waiting for transfers between devices, local(): entity_grad = lax.psum(entity_acc, 'rel')  51.3 us
    all_to_all x1, waiting for transfers between devices, local(): lax.all_to_all(slot_grads.astype(jnp.bfloat16), 'ent', split_axis=1, conc...  27.4 us
    all_to_all x1, waiting for transfers between devices, local(): lax.all_to_all(wanted, 'ent', split_axis=0, concat_axis=1, tiled=True)  25.4 us
    dot_general x9, matrix products, pick_block(): jnp.dot(one_hot, source_table, preferred_element_type=jnp.float32)  17.8 us
    all_to_all x1, starting transfers between devices, local(): lax.all_to_all(request_rows, 'ent', split_axis=1, concat_axis=0, tiled=True)  12.1 us
    scatter-add x1, other arithmetic, owner_add(): return start_value.at[indices].add(gradients)  12 us
    all_to_all x1, waiting for transfers between devices, local(): lax.all_to_all(request_rows, 'ent', split_axis=1, concat_axis=0, tiled=True)  8.54 us
  transfers between devices with their start and end apart: 5, of which 5 were waited for; matrix products, arithmetic and copies ran while one was open for 5% of the time, Pallas kernels for 0%

commit v1 on v0

--- a/solution.py
+++ b/solution.py
@@ -148,7 +148,7 @@
     entity_acc = entity_acc + owner_add(
         owner_lists.reshape(-1), returned.reshape(-1, feature_width), entity_count
     )
-    entity_grad = lax.psum(entity_acc, "rel")
+    entity_grad = jnp.sum(lax.all_gather(entity_acc, "rel"), axis=0)
     relation_grad = lax.psum(relation_acc, "ent")
     return (entity_grad, relation_grad)
 

time: 384 us -> 371 us (0.966)
  waiting for transfers between devices: 263 us -> 246 us
    psum x1 -> x0, waiting for transfers between devices: 51.3 us -> none  [local(): entity_grad = lax.psum(entity_acc, 'rel')]
    all_gather x0 -> x1, waiting for transfers between devices: none -> 45.9 us  [local(): entity_grad = jnp.sum(lax.all_gather(entity_acc, 'rel'), axis=0)]
    psum x1, waiting for transfers between devices: 151 us -> 138 us  [local(): relation_grad = lax.psum(relation_acc, 'ent')]
  transfers between devices with their start and end apart: 5 -> 5, of which waited for: 5 -> 5; matrix products, arithmetic and copies ran while one was open for 5% -> 2% of each run, Pallas kernels for 0% -> 0%
where the time goes in v1:
time: 371 us; the launch traced here: 369 us
  waiting for transfers between devices  246 us (66%)
  matrix products  53.8 us (15%)
  starting transfers between devices  24.4 us (7%)
  other arithmetic  20.1 us (5%)
  between operations  15.7 us (4%)
  local copies, waits for them, and re-layouts  8.78 us (2%)
    psum x1, waiting for transfers between devices, local(): relation_grad = lax.psum(relation_acc, 'ent')  138 us
    all_gather x1, waiting for transfers between devices, local(): entity_grad = jnp.sum(lax.all_gather(entity_acc, 'rel'), axis=0)  45.9 us
    all_to_all x1, waiting for transfers between devices, local(): lax.all_to_all(slot_grads.astype(jnp.bfloat16), 'ent', split_axis=1, conc...  28 us
    all_to_all x1, waiting for transfers between devices, local(): lax.all_to_all(wanted, 'ent', split_axis=0, concat_axis=1, tiled=True)  25.4 us
    dot_general x9, matrix products, pick_block(): jnp.dot(one_hot, source_table, preferred_element_type=jnp.float32)  17.8 us
    all_to_all x1, starting transfers between devices, local(): lax.all_to_all(request_rows, 'ent', split_axis=1, concat_axis=0, tiled=True)  12.1 us
    scatter-add x1, other arithmetic, owner_add(): return start_value.at[indices].add(gradients)  12 us
    all_to_all x1, waiting for transfers between devices, local(): lax.all_to_all(request_rows, 'ent', split_axis=1, concat_axis=0, tiled=True)  8.54 us
  transfers between devices with their start and end apart: 5, of which 5 were waited for; matrix products, arithmetic and copies ran while one was open for 2% of the time, Pallas kernels for 0%

profile of v1, /device:TPU:8, one launch (start us, length us, event | category | flops | bytes accessed | tf_op | source)
XLA Modules:
  0.0 369.3 jit_solution(6209630855340743027)
XLA Ops:
  9.4 12.1 %all-to-all-start = ((s32[1,64,32]{2,0,1:T(1,128)}), s32[1,64,32]{2,0,1:T(1,128)S(1)}, u32[]{:S(2)}, u32[]{:S(2)}) async-start(s32[1,64,32]{2,0,1:T(1,128)} %copy.20), calls=%async_computation | async-start | bytes 65536 | tf_op jit(solution)/shard_map/all_to_all | solution.py:48
  21.5 8.5 %all-to-all-done = s32[1,64,32]{2,0,1:T(1,128)S(1)} async-done(((s32[1,64,32]{2,0,1:T(1,128)}), s32[1,64,32]{2,0,1:T(1,128)S(1)}, u32[]{:S(2)}, u32[]{:S(2)}) %all-to-all-start) | async-done | bytes 8224 | tf_op jit(solution)/shard_map/all_to_all | solution.py:48
  31.4 16.5 %while.32 = (s32[]{:T(128)}, bf16[8,256,256]{2,1,0:T(8,128)(2,1)}, s32[8,256]{1,0:T(8,128)S(1)}, bf16[1024,256]{1,0:T(8,128)(2,1)}, s32[]{:T(128)}) while((s32[]{:T(128)}, bf16[8,256,256]{2,1,0:T(8,128)(2,1)}, s32[8,256]{1,0:T(8,128)S(1)}, bf16[1024,256]{1,0:T(8,128)(2,1)}, s32[]{:T(128)}) %tuple.56), condition=%wide.region_1.2_spmd.clone, body=%wide.region_0.1_spmd.clone.sunk | while | flops 134545408 | bytes 658509 | solution.py:20
  31.4 2.1 fusion.90
  33.5 2.0 fusion.90
  35.5 2.1 fusion.90
  37.6 2.1 fusion.90
  39.6 2.1 fusion.90
  41.7 2.0 fusion.90
  45.8 2.1 fusion.90
  47.9 6.5 %all-to-all-start.1 = ((bf16[64,1,32,256]{3,2,1,0:T(8,128)(2,1)}), bf16[64,1,32,256]{3,2,1,0:T(8,128)(2,1)}, u32[]{:S(2)}, u32[]{:S(2)}) async-start(bf16[64,1,32,256]{3,2,1,0:T(8,128)(2,1)} %bitcast.1), calls=%async_computation.1 | async-start | bytes 2097152 | tf_op jit(solution)/shard_map/all_to_all | solution.py:52
  57.8 25.4 %all-to-all-done.1 = bf16[64,1,32,256]{3,2,1,0:T(8,128)(2,1)} async-done(((bf16[64,1,32,256]{3,2,1,0:T(8,128)(2,1)}), bf16[64,1,32,256]{3,2,1,0:T(8,128)(2,1)}, u32[]{:S(2)}, u32[]{:S(2)}) %all-to-all-start.1) | async-done | bytes 1048608 | tf_op jit(solution)/shard_map/all_to_all | solution.py:52
  83.1 38.9 %while.33 = (s32[]{:T(128)}, f32[2048,256]{1,0:T(8,128)S(1)}, f32[1024,256]{1,0:T(8,128)S(1)}, f32[256,256]{1,0:T(8,128)S(1)}, f32[8,8,32,32]{2,3,0,1:T(8,128)},...) while((s32[]{:T(128)}, f32[2048,256]{1,0:T(8,128)S(1)}, ...), condition=%wide.region_6.7_spmd.clone, body=%wide.region_2.6_spmd.clone.sunk | while | flops 1016077568 | bytes 14733582 | solution.py:137
  87.5 2.1 fusion.111
  97.2 2.1 fusion.111
  106.9 2.1 fusion.111
  116.7 2.1 fusion.111
  123.2 5.7 %all-to-all-start.2 = ((bf16[1,64,32,256]{3,2,0,1:T(8,128)(2,1)}), bf16[1,64,32,256]{3,2,0,1:T(8,128)(2,1)S(1)}, u32[]{:S(2)}, u32[]{:S(2)}) async-start(bf16[1,64,32,256]{3,2,0,1:T(8,128)(2,1)} %bitcast.125), calls=%async_computation.2 | async-start | bytes 2097152 | tf_op jit(solution)/shard_map/all_to_all | solution.py:145
  129.7 28.0 %all-to-all-done.2 = bf16[1,64,32,256]{3,2,0,1:T(8,128)(2,1)S(1)} async-done(((bf16[1,64,32,256]{3,2,0,1:T(8,128)(2,1)}), bf16[1,64,32,256]{3,2,0,1:T(8,128)(2,1)S(1)}, u32[]{:S(2)}, u32[]{:S(2)}) %all-to-all-start.2) | async-done | bytes 1048608 | tf_op jit(solution)/shard_map/all_to_all | solution.py:145
  157.7 12.0 %scatter_custom_fusion = f32[1024,256]{1,0:T(8,128)S(1)} fusion(f32[1024,256]{1,0:T(8,128)S(1)} %convolution_add_fusion.4, s32[2048]{0:T(1024)S(1)} %bitcast.140, bf16[2048,256]{1,0:T(8,128)(2,1)S(1)} %bitcast.127), kind=kCustom, calls=%fused_computation.57 | custom fusion | flops 1048576 | bytes 2097152 | tf_op jit(solution)/shard_map/scatter-add | solution.py:26
  172.1 45.9 %all-gather.3.cloned.1.call-done = f32[4096,256]{1,0:T(8,128)} async-done(((f32[1024,256]{1,0:T(8,128)}), f32[4096,256]{1,0:T(8,128)}) %all-gather.3.cloned.1.call-update) | async-done | bytes 4194320 | tf_op jit(solution)/shard_map/all_gather | solution.py:151
  218.0 3.6 reduce_sum.36
  221.6 137.9 %all-reduce.2.cloned.1.call-done = f32[8,8,32,32]{3,2,1,0:T(8,128)} async-done(((f32[8,8,32,32]{3,2,1,0:T(8,128)}), f32[8,8,32,32]{3,2,1,0:T(8,128)}) %all-reduce.2.cloned.1.call-update) | async-done | bytes 262160 | tf_op jit(solution)/shard_map/psum | solution.py:152
  359.6 2.3 copy.50
  (129 shorter events, 42.3 us)
Async XLA Ops:
  9.4 20.7 %all-to-all-start = ((s32[1,64,32]{2,0,1:T(1,128)}), s32[1,64,32]{2,0,1:T(1,128)S(1)}, u32[]{:S(2)}, u32[]{:S(2)}) async-start(s32[1,64,32]{2,0,1:T(1,128)} %copy.20), calls=%async_computation | async-start | bytes 65536 | tf_op jit(solution)/shard_map/all_to_all | solution.py:48
  30.1 1.3 copy-start.5
  47.9 6.5 %copy-start.7 = (s32[1024]{0:T(1024)S(1)}, s32[1024]{0:T(1024)}, u32[]{:S(2)}) copy-start(s32[1024]{0:T(1024)} %param.14) | copy-start | bytes 12292
  47.9 6.5 %copy-start.8 = (s32[1024]{0:T(1024)S(1)}, s32[1024]{0:T(1024)}, u32[]{:S(2)}) copy-start(s32[1024]{0:T(1024)} %param.15) | copy-start | bytes 12292
  47.9 6.6 %copy-start.9 = (s32[1024]{0:T(1024)S(1)}, s32[1024]{0:T(1024)}, u32[]{:S(2)}) copy-start(s32[1024]{0:T(1024)} %param.16) | copy-start | bytes 12292
  47.9 35.3 %all-to-all-start.1 = ((bf16[64,1,32,256]{3,2,1,0:T(8,128)(2,1)}), bf16[64,1,32,256]{3,2,1,0:T(8,128)(2,1)}, u32[]{:S(2)}, u32[]{:S(2)}) async-start(bf16[64,1,32,256]{3,2,1,0:T(8,128)(2,1)} %bitcast.1), calls=%async_computation.1 | async-start | bytes 2097152 | tf_op jit(solution)/shard_map/all_to_all | solution.py:52
  87.2 2.6 copy-start.4
  87.5 2.8 copy-start
  91.2 1.7 copy-start.1
  96.9 2.6 copy-start.4
  97.2 2.8 copy-start
  100.9 1.7 copy-start.1
  106.7 2.6 copy-start.4
  106.9 2.8 copy-start
  110.7 1.7 copy-start.1
  116.4 2.6 copy-start.4
  116.7 2.8 copy-start
  120.4 1.7 copy-start.1
  122.1 6.9 %copy-start.6 = (s32[1,64,32]{2,0,1:T(1,128)S(1)}, s32[1,64,32]{2,0,1:T(1,128)}, u32[]{:S(2)}) copy-start(s32[1,64,32]{2,0,1:T(1,128)} %copy-done.5) | copy-start | bytes 24580
  122.1 7.0 %copy-start.10 = (s32[256]{0:T(256)S(1)}, s32[256]{0:T(256)}, u32[]{:S(2)}) copy-start(s32[256]{0:T(256)} %param.18) | copy-start | bytes 3076
  123.2 34.5 %all-to-all-start.2 = ((bf16[1,64,32,256]{3,2,0,1:T(8,128)(2,1)}), bf16[1,64,32,256]{3,2,0,1:T(8,128)(2,1)S(1)}, u32[]{:S(2)}, u32[]{:S(2)}) async-start(bf16[1,64,32,256]{3,2,0,1:T(8,128)(2,1)} %bitcast.125), calls=%async_computation.2 | async-start | bytes 2097152 | tf_op jit(solution)/shard_map/all_to_all | solution.py:145
  128.9 89.1 %all-gather.3.cloned.1.call-start = ((), (), s32[]{:S(2)}) async-start(), calls=%async_computation.4 | async-start | bytes 5242880 | tf_op jit(solution)/shard_map/all_gather | solution.py:151
  129.6 41.1 %copy-start.2 = (f32[8,8,32,32]{2,3,0,1:T(8,128)S(1)}, f32[8,8,32,32]{2,3,0,1:T(8,128)}, u32[]{:S(2)}) copy-start(f32[8,8,32,32]{2,3,0,1:T(8,128)} %get-tuple-element.138) | copy-start | bytes 786436
  170.7 188.9 %all-reduce.2.cloned.1.call-start = ((), (), s32[]{:S(2)}) async-start(), calls=%async_computation.3 | async-start | bytes 2097152 | tf_op jit(solution)/shard_map/psum | solution.py:152
  (1 other events, 1.0 us)
Sparse Core Ops, SparseCore 0:
  170.8 47.1 all-gather.2
Sparse Core Ops, SparseCore 1:
  175.2 184.3 all-reduce.1
